TPU v7x, 32 devices: a whole 2x2x4 slice. The times are simulated.
32 devices in a mesh: dp: 2 (over x), tok: 4 (over z), mp: 4 (over y, core).
Axes of the slice: x: 2, y: 2, z: 4, core: 2. Of those that a mesh axis runs over, the one named last changes fastest.
Arguments:
- tokens: bfloat16 [16384, 1024], P(('dp', 'tok'), 'mp'), may hold values from -6 to 6
- in_weight: bfloat16 [1024, 3, 1024], P(('dp', 'tok'), None, 'mp'), may hold values from -0.1875 to 0.1875
- conv_kernel: bfloat16 [3, 1024], P(None, 'mp'), may hold values from -2.5 to 2.5
- out_weight: bfloat16 [1024, 1024], P('mp', ('dp', 'tok')), may hold values from -0.1875 to 0.1875
- gate_weight: bfloat16 [1024, 4608], P(('dp', 'tok'), 'mp'), may hold values from -0.1875 to 0.1875
- up_weight: bfloat16 [1024, 4608], P(('dp', 'tok'), 'mp'), may hold values from -0.1875 to 0.1875
- down_weight: bfloat16 [4608, 1024], P('mp', ('dp', 'tok')), may hold values from -0.09375 to 0.09375
- mixer_norm_gain: float32 [1024], replicated, may hold values from 0.5 to 1.5
- gain_ffn: float32 [1024], replicated, may hold values from 0.5 to 1.5
- cotangent: bfloat16 [16384, 1024], P(('dp', 'tok'), 'mp'), may hold values from -6 to 6
Outputs:
- mixed: bfloat16 [16384, 1024], P(('dp', 'tok'), 'mp')
- input_token_gradient: float32 [16384, 1024], P(('dp', 'tok'), 'mp')
- grad_in_weight: float32 [1024, 3, 1024], P(('dp', 'tok'), None, 'mp')
- grad_conv_kernel: float32 [3, 1024], P(None, 'mp')
- grad_out_weight: float32 [1024, 1024], P('mp', ('dp', 'tok'))
- grad_gate_weight: float32 [1024, 4608], P(('dp', 'tok'), 'mp')
- grad_up_weight: float32 [1024, 4608], P(('dp', 'tok'), 'mp')
- grad_down_weight: float32 [4608, 1024], P('mp', ('dp', 'tok'))
- grad_gain_mix: float32 [1024], P('mp')
- grad_gain_ffn: float32 [1024], P('mp')
All inputs are finite; a program needn't handle non-finite values.
Results may differ from a plain program's by a relative error of at most 0.011.
Values may be sent and summed in bfloat16 or wider, within the bound.
No kernel may reach another device: no remote copies, remote signals or barrier semaphores. Data moves between devices by JAX's collectives and lax.ppermute only.
A program may use at most 192 MiB of HBM per device.

v0:
```python
import jax
import jax.numpy as jnp
from jax import lax
from jax.sharding import PartitionSpec as P

eps_norm = 1e-05


def passed_along(block, axis, distance):
    devices = range(lax.axis_size(axis))
    route = [(i - distance, i) for i in devices if i - distance in devices]
    return lax.ppermute(block, axis, route)


def collect_rows(values):
    return lax.all_gather(values, "mp", axis=1, tiled=True)


def sum_features(values):
    return lax.psum_scatter(values, "mp", scatter_dimension=1, tiled=True)


def total_row_count(values):
    return lax.psum(values, "mp")


def body(
    tokens,
    in_weight,
    conv_kernel,
    out_weight,
    gate_weight,
    up_weight,
    down_weight,
    mixer_norm_gain,
    gain_ffn,
    cotangent,
):
    f32 = jnp.float32
    brain_float_sixteen = jnp.bfloat16
    feature_width = tokens.shape[1]
    hidden_model_width = feature_width * lax.axis_size("mp")
    start_position = lax.axis_index("mp") * feature_width
    mix_slice = lax.dynamic_slice_in_dim(mixer_norm_gain, start_position, feature_width)
    feedforward_portion = lax.dynamic_slice_in_dim(gain_ffn, start_position, feature_width)
    w_in, w_out, w_gate, w_up, w_down = (
        lax.all_gather(in_weight, ("dp", "tok"), axis=0, tiled=True),
        lax.all_gather(out_weight, ("dp", "tok"), axis=1, tiled=True),
        lax.all_gather(gate_weight, ("dp", "tok"), axis=0, tiled=True),
        lax.all_gather(up_weight, ("dp", "tok"), axis=0, tiled=True),
        lax.all_gather(down_weight, ("dp", "tok"), axis=1, tiled=True),
    )
    taps = conv_kernel.astype(f32)
    complete_inputs = collect_rows(tokens).astype(f32)
    mixer_inverse_norm = lax.rsqrt(
        jnp.mean(complete_inputs * complete_inputs, -1, keepdims=True) + eps_norm
    )
    complete_normalized = complete_inputs * mixer_inverse_norm
    mixer_hidden = (complete_normalized * mixer_norm_gain).astype(brain_float_sixteen)
    proj = jnp.einsum("td,dkc->tkc", mixer_hidden, w_in, preferred_element_type=f32)
    gate_b = proj[:, 0]
    gate_c = proj[:, 1]
    gate_x = proj[:, 2]
    gated = (gate_b * gate_x).astype(brain_float_sixteen)
    edge = passed_along(gated[-2:], "tok", 1)
    extended = jnp.concatenate([edge, gated], 0).astype(f32)
    rows_count = gated.shape[0]
    conv = (
        taps[0] * extended[0:rows_count]
        + taps[1] * extended[1 : rows_count + 1]
        + taps[2] * extended[2:]
    )
    mixed_in = (gate_c * conv).astype(brain_float_sixteen)
    residual_stream = tokens.astype(f32) + sum_features(
        jnp.dot(mixed_in, w_out, preferred_element_type=f32)
    )
    square_sum = total_row_count(jnp.sum(residual_stream * residual_stream, -1))
    feedforward_inverse_norm = lax.rsqrt(square_sum[:, None] / hidden_model_width + eps_norm)
    feedforward_normalized = residual_stream * feedforward_inverse_norm
    feedforward_hidden = collect_rows(
        (feedforward_normalized * feedforward_portion).astype(brain_float_sixteen)
    )
    gate = jnp.dot(feedforward_hidden, w_gate, preferred_element_type=f32)
    upper = jnp.dot(feedforward_hidden, w_up, preferred_element_type=f32)
    sigma = jax.nn.sigmoid(gate)
    silu_gate = gate * sigma
    hidden = (silu_gate * upper).astype(brain_float_sixteen)
    result = residual_stream + sum_features(jnp.dot(hidden, w_down, preferred_element_type=f32))
    mixed = result.astype(brain_float_sixteen)
    cot_full = collect_rows(cotangent)
    dhidden = jnp.einsum("td,fd->tf", cot_full, w_down, preferred_element_type=f32)
    grad_down = jnp.einsum("tf,td->fd", hidden, cot_full, preferred_element_type=f32)
    dgate = (dhidden * upper * sigma * (1.0 + gate * (1.0 - sigma))).astype(brain_float_sixteen)
    dupper = (dhidden * silu_gate).astype(brain_float_sixteen)
    grad_gate = jnp.einsum("td,tf->df", feedforward_hidden, dgate, preferred_element_type=f32)
    grad_up = jnp.einsum("td,tf->df", feedforward_hidden, dupper, preferred_element_type=f32)
    back_ffn = jnp.einsum("tf,df->td", dgate, w_gate, preferred_element_type=f32) + jnp.einsum(
        "tf,df->td", dupper, w_up, preferred_element_type=f32
    )
    feedforward_hidden_gradient = sum_features(back_ffn)
    feedforward_gain_gradient = jnp.sum(feedforward_hidden_gradient * feedforward_normalized, 0)
    feedforward_scaled_input = feedforward_hidden_gradient * feedforward_portion
    feedforward_dot_product = total_row_count(
        jnp.sum(feedforward_scaled_input * feedforward_normalized, -1)
    )
    residual_gradient = cotangent.astype(f32) + feedforward_inverse_norm * (
        feedforward_scaled_input
        - feedforward_normalized * (feedforward_dot_product[:, None] / hidden_model_width)
    )
    dresid_full = collect_rows(residual_gradient.astype(brain_float_sixteen))
    grad_out = jnp.einsum("tc,td->cd", mixed_in, dresid_full, preferred_element_type=f32)
    dmixed = jnp.einsum("td,cd->tc", dresid_full, w_out, preferred_element_type=f32)
    dconv = (dmixed * gate_c).astype(brain_float_sixteen)
    dgate_c = dmixed * conv
    after = passed_along(dconv[:2], "tok", -1)
    dconv_ext = jnp.concatenate([dconv, after], 0).astype(f32)
    dconv_own = dconv_ext[0:rows_count]
    grad_taps = jnp.stack(
        [
            jnp.sum(dconv_own * extended[0:rows_count], 0),
            jnp.sum(dconv_own * extended[1 : rows_count + 1], 0),
            jnp.sum(dconv_own * extended[2:], 0),
        ],
        0,
    )
    dgated = taps[2] * dconv_own + taps[1] * dconv_ext[1 : rows_count + 1] + taps[0] * dconv_ext[2:]
    dproj = jnp.stack([dgated * gate_x, dgate_c, dgated * gate_b], 1).astype(brain_float_sixteen)
    grad_in = jnp.einsum("td,tkc->dkc", mixer_hidden, dproj, preferred_element_type=f32)
    mixer_hidden_gradient = sum_features(
        jnp.einsum("tkc,dkc->td", dproj, w_in, preferred_element_type=f32)
    )
    mixer_normalized = lax.dynamic_slice_in_dim(
        complete_normalized, start_position, feature_width, 1
    )
    mixer_gain_gradient = jnp.sum(mixer_hidden_gradient * mixer_normalized, 0)
    mixer_scaled_input = mixer_hidden_gradient * mix_slice
    mixer_dot_product = total_row_count(jnp.sum(mixer_scaled_input * mixer_normalized, -1))
    input_token_gradient = residual_gradient + mixer_inverse_norm * (
        mixer_scaled_input - mixer_normalized * (mixer_dot_product[:, None] / hidden_model_width)
    )
    grad_taps, mixer_gain_gradient, feedforward_gain_gradient = lax.psum(
        (grad_taps, mixer_gain_gradient, feedforward_gain_gradient), ("dp", "tok")
    )
    g_in, g_out, g_gate, g_up, g_down = (
        lax.psum_scatter(grad_in, ("dp", "tok"), scatter_dimension=0, tiled=True),
        lax.psum_scatter(grad_out, ("dp", "tok"), scatter_dimension=1, tiled=True),
        lax.psum_scatter(grad_gate, ("dp", "tok"), scatter_dimension=0, tiled=True),
        lax.psum_scatter(grad_up, ("dp", "tok"), scatter_dimension=0, tiled=True),
        lax.psum_scatter(grad_down, ("dp", "tok"), scatter_dimension=1, tiled=True),
    )
    return (
        mixed,
        input_token_gradient,
        g_in,
        grad_taps,
        g_out,
        g_gate,
        g_up,
        g_down,
        mixer_gain_gradient,
        feedforward_gain_gradient,
    )


def solution(mesh):
    return jax.shard_map(
        body,
        mesh=mesh,
        in_specs=(
            P(("dp", "tok"), "mp"),
            P(("dp", "tok"), None, "mp"),
            P(None, "mp"),
            P("mp", ("dp", "tok")),
            P(("dp", "tok"), "mp"),
            P(("dp", "tok"), "mp"),
            P("mp", ("dp", "tok")),
            P(),
            P(),
            P(("dp", "tok"), "mp"),
        ),
        out_specs=(
            P(("dp", "tok"), "mp"),
            P(("dp", "tok"), "mp"),
            P(("dp", "tok"), None, "mp"),
            P(None, "mp"),
            P("mp", ("dp", "tok")),
            P(("dp", "tok"), "mp"),
            P(("dp", "tok"), "mp"),
            P("mp", ("dp", "tok")),
            P("mp"),
            P("mp"),
        ),
        check_vma=False,
    )
```

profile of v0, /device:TPU:0, one launch (start us, length us, event | category | flops | bytes accessed | tf_op | source)
XLA Modules:
  0.0 1189.8 jit_solution(4125879485622382611)
XLA Ops:
  8.7 30.9 %all_gather.29 = bf16[256,1024]{1,0:T(8,128)(2,1)S(1)} all-gather(bf16[256,128]{1,0:T(8,128)(2,1)} %param.13), channel_id=1, replica_groups=mesh['dp'=2,'tok'=4,'mp'=4] {'dp','tok'}, dimensions={1}, use_global_device_ids=true | all-gather | bytes 589824 | tf_op jit(solution)/shard_map/all_gather | solution.py:48
  50.4 43.3 %all-gather.11.cloned.1.call-done = bf16[1024,3,256]{2,0,1:T(8,128)(2,1)} async-done(((bf16[128,3,256]{2,0,1:T(8,128)(2,1)}), bf16[1024,3,256]{2,0,1:T(8,128)(2,1)}) %all-gather.11.cloned.1.call-update) | async-done | bytes 1572880 | tf_op jit(solution)/shard_map/all_gather | solution.py:47
  114.0 69.7 %reduce-scatter.10.cloned.1.call-done = f32[2048,256]{1,0:T(8,128)} async-done(((f32[2048,1024]{1,0:T(8,128)}), f32[2048,256]{1,0:T(8,128)}) %reduce-scatter.10.cloned.1.call-update) | async-done | bytes 2097168 | tf_op jit(solution)/shard_map/reduce_scatter | solution.py:20
  198.2 39.8 %all-gather.15.cloned.1.call-done = bf16[1024,1152]{1,0:T(8,128)(2,1)} async-done(((bf16[128,1152]{1,0:T(8,128)(2,1)}), bf16[1024,1152]{1,0:T(8,128)(2,1)}) %all-gather.15.cloned.1.call-update) | async-done | bytes 2359312 | tf_op jit(solution)/shard_map/all_gather | solution.py:49
  238.0 35.7 %all-gather.13.cloned.1.call-done = bf16[2048,1024]{1,0:T(8,128)(2,1)} async-done(((bf16[2048,256]{1,0:T(8,128)(2,1)}), bf16[2048,1024]{1,0:T(8,128)(2,1)}) %all-gather.13.cloned.1.call-update) | async-done | bytes 4194320 | tf_op jit(solution)/shard_map/all_gather | solution.py:16
  273.6 10.2 fusion.18
  283.8 44.0 %all-gather.17.cloned.1.call-done = bf16[1024,1152]{1,0:T(8,128)(2,1)} async-done(((bf16[128,1152]{1,0:T(8,128)(2,1)}), bf16[1024,1152]{1,0:T(8,128)(2,1)}) %all-gather.17.cloned.1.call-update) | async-done | bytes 2359312 | tf_op jit(solution)/shard_map/all_gather | solution.py:50
  327.9 10.2 fusion.19
  338.1 44.3 %all-gather.19.cloned.1.call-done = bf16[1152,1024]{1,0:T(8,128)(2,1)} async-done(((bf16[1152,128]{1,0:T(8,128)(2,1)}), bf16[1152,1024]{1,0:T(8,128)(2,1)}) %all-gather.19.cloned.1.call-update) | async-done | bytes 2359312 | tf_op jit(solution)/shard_map/all_gather | solution.py:51
  382.4 34.9 %all-gather.21.cloned.1.call-done = bf16[2048,1024]{1,0:T(8,128)(2,1)} async-done(((bf16[2048,256]{1,0:T(8,128)(2,1)}), bf16[2048,1024]{1,0:T(8,128)(2,1)}) %all-gather.21.cloned.1.call-update) | async-done | bytes 4194320 | tf_op jit(solution)/shard_map/all_gather | solution.py:16
  417.3 17.9 %multiply_convert_fusion = (bf16[2048,1152]{1,0:T(8,128)(2,1)}, bf16[2048,1152]{1,0:T(8,128)(2,1)}, bf16[2048,1152]{1,0:T(8,128)(2,1)}) fusion(f32[2048,1152]{1,0:T(8,128)} %fusion.18, f32[2048,1152]{1,0:T(8,128)} %fusion.19, bf16[2048,1024]{1,0:T(8,128)(2,1)} %all-gather.21.cloned.1.call-done, bf16[1152,1024]{1,0:T(8,128)(2,1)} %all-gather.19.cloned.1.call-done), kind=kOutput, calls=%fused_computation.2 | convolution fusion | flops 4867227648 | bytes 39583744 | tf_op jit(solution)/shard_map/td,fd->tf/dot_general | solution.py:91
  451.8 71.8 %reduce-scatter.14.cloned.1.call-done = f32[2048,256]{1,0:T(8,128)} async-done(((f32[2048,1024]{1,0:T(8,128)}), f32[2048,256]{1,0:T(8,128)}) %reduce-scatter.14.cloned.1.call-update) | async-done | bytes 2097168 | tf_op jit(solution)/shard_map/reduce_scatter | solution.py:20
  536.0 36.2 %all-gather.23.cloned.1.call-done = bf16[2048,1024]{1,0:T(8,128)(2,1)} async-done(((bf16[2048,256]{1,0:T(8,128)(2,1)}), bf16[2048,1024]{1,0:T(8,128)(2,1)}) %all-gather.23.cloned.1.call-update) | async-done | bytes 4194320 | tf_op jit(solution)/shard_map/all_gather | solution.py:16
  593.4 10.6 fusion.20
  604.1 11.5 fusion.24
  615.7 10.6 fusion.25
  626.4 9.8 fusion.26
  667.0 22.4 %all-reduce = (f32[3,256]{1,0:T(4,128)}, f32[256]{0:T(256)}, f32[256]{0:T(256)}) all-reduce(f32[3,256]{1,0:T(4,128)S(1)} %pad_maximum_fusion.3, f32[256]{0:T(256)S(1)} %get-tuple-element.10, f32[256]{0:T(256)S(1)} %get-tuple-element.15), channel_id=1, replica_groups=mesh['dp'=2,'tok'=4,'mp'=4] {'dp','tok'}, use_global_device_ids=true, to_apply=%region_15.0 | all-reduce | flops 1280 | bytes 10240 | tf_op jit(solution)/shard_map/psum | solution.py:141
  695.7 43.2 %reduce-scatter.12.cloned.1.call-done = f32[2048,256]{1,0:T(8,128)} async-done(((f32[2048,1024]{1,0:T(8,128)}), f32[2048,256]{1,0:T(8,128)}) %reduce-scatter.12.cloned.1.call-update) | async-done | bytes 2097168 | tf_op jit(solution)/shard_map/reduce_scatter | solution.py:20
  744.1 94.0 %reduce-scatter.22.cloned.1.call-done = f32[128,1152]{1,0:T(8,128)} async-done(((f32[1024,1152]{1,0:T(8,128)}), f32[128,1152]{1,0:T(8,128)}) %reduce-scatter.22.cloned.1.call-update) | async-done | bytes 589840 | tf_op jit(solution)/shard_map/reduce_scatter | solution.py:147
  838.1 99.3 %reduce-scatter.24.cloned.1.call-done = f32[128,1152]{1,0:T(8,128)} async-done(((f32[1024,1152]{1,0:T(8,128)}), f32[128,1152]{1,0:T(8,128)}) %reduce-scatter.24.cloned.1.call-update) | async-done | bytes 589840 | tf_op jit(solution)/shard_map/reduce_scatter | solution.py:148
  937.4 99.6 %reduce-scatter.26.cloned.1.call-done = f32[1152,128]{1,0:T(8,128)} async-done(((f32[1152,1024]{1,0:T(8,128)}), f32[1152,128]{1,0:T(8,128)}) %reduce-scatter.26.cloned.1.call-update) | async-done | bytes 589840 | tf_op jit(solution)/shard_map/reduce_scatter | solution.py:149
  1036.9 67.6 %reduce-scatter.20.cloned.1.call-done = f32[256,128]{1,0:T(8,128)} async-done(((f32[256,1024]{1,0:T(8,128)}), f32[256,128]{1,0:T(8,128)}) %reduce-scatter.20.cloned.1.call-update) | async-done | bytes 131088 | tf_op jit(solution)/shard_map/reduce_scatter | solution.py:146
  1104.6 78.4 %reduce-scatter.18.cloned.1.call-done = f32[128,3,256]{2,0,1:T(8,128)} async-done(((f32[1024,3,256]{2,0,1:T(8,128)}), f32[128,3,256]{2,0,1:T(8,128)}) %reduce-scatter.18.cloned.1.call-update) | async-done | bytes 393232 | tf_op jit(solution)/shard_map/reduce_scatter | solution.py:145
  (113 shorter events, 139.3 us)
Async XLA Ops:
  7.2 40.1 %all-gather.9.cloned.1.call-start = ((), (), s32[]{:S(2)}) async-start(), calls=%async_computation.9 | async-start | bytes 5242880 | tf_op jit(solution)/shard_map/all_gather | solution.py:16
  7.9 85.8 %all-gather.11.cloned.1.call-start = ((), (), s32[]{:S(2)}) async-start(), calls=%async_computation.10 | async-start | bytes 1769472 | tf_op jit(solution)/shard_map/all_gather | solution.py:47
  8.7 85.0 %copy-start.11 = (f32[1024]{0:T(1024)S(1)}, f32[1024]{0:T(1024)}, u32[]{:S(2)}) copy-start(f32[1024]{0:T(1024)} %param.17) | copy-start | bytes 12292
  8.7 175.0 %reduce-scatter.10.cloned.1.call-start = ((), (), s32[]{:S(2)}) async-start(), calls=%async_computation.11 | async-start | bytes 10485760 | tf_op jit(solution)/shard_map/reduce_scatter | solution.py:20
  39.6 67.5 %copy-start.7 = (bf16[256,1024]{1,0:T(8,128)(2,1)}, bf16[256,1024]{1,0:T(8,128)(2,1)S(1)}, u32[]{:S(2)}) copy-start(bf16[256,1024]{1,0:T(8,128)(2,1)S(1)} %all_gather.29) | copy-start | bytes 1572868
  99.7 5.1 collective-permute-start
  112.6 71.1 %copy-start.6 = (bf16[2048,256]{1,0:T(8,128)(2,1)S(1)}, bf16[2048,256]{1,0:T(8,128)(2,1)}, u32[]{:S(2)}) copy-start(bf16[2048,256]{1,0:T(8,128)(2,1)} %param.10) | copy-start | bytes 3145732
  112.6 125.4 %all-gather.15.cloned.1.call-start = ((), (), s32[]{:S(2)}) async-start(), calls=%async_computation.13 | async-start | bytes 2654208 | tf_op jit(solution)/shard_map/all_gather | solution.py:49
  113.2 160.4 %all-gather.13.cloned.1.call-start = ((), (), s32[]{:S(2)}) async-start(), calls=%async_computation.12 | async-start | bytes 5242880 | tf_op jit(solution)/shard_map/all_gather | solution.py:16
  195.8 132.1 %all-gather.17.cloned.1.call-start = ((), (), s32[]{:S(2)}) async-start(), calls=%async_computation.14 | async-start | bytes 2654208 | tf_op jit(solution)/shard_map/all_gather | solution.py:50
  196.4 186.1 %all-gather.19.cloned.1.call-start = ((), (), s32[]{:S(2)}) async-start(), calls=%async_computation.15 | async-start | bytes 2654208 | tf_op jit(solution)/shard_map/all_gather | solution.py:51
  197.1 220.2 %all-gather.21.cloned.1.call-start = ((), (), s32[]{:S(2)}) async-start(), calls=%async_computation.17 | async-start | bytes 5242880 | tf_op jit(solution)/shard_map/all_gather | solution.py:16
  197.9 325.8 %reduce-scatter.14.cloned.1.call-start = ((), (), s32[]{:S(2)}) async-start(), calls=%async_computation.18 | async-start | bytes 10485760 | tf_op jit(solution)/shard_map/reduce_scatter | solution.py:20
  451.8 80.7 %copy-start.2 = (bf16[2048,256]{1,0:T(8,128)(2,1)S(1)}, bf16[2048,256]{1,0:T(8,128)(2,1)}, u32[]{:S(2)}) copy-start(bf16[2048,256]{1,0:T(8,128)(2,1)} %param.19) | copy-start | bytes 3145732
  451.8 120.4 %all-gather.23.cloned.1.call-start = ((), (), s32[]{:S(2)}) async-start(), calls=%async_computation.19 | async-start | bytes 5242880 | tf_op jit(solution)/shard_map/all_gather | solution.py:16
  535.9 128.4 %reduce-scatter.16.cloned.1.call-start = ((), (), s32[]{:S(2)}) async-start(), calls=%async_computation.20 | async-start | bytes 10485760 | tf_op jit(solution)/shard_map/reduce_scatter | solution.py:20
  578.4 5.6 collective-permute-start.1
  593.3 145.6 %reduce-scatter.12.cloned.1.call-start = ((), (), s32[]{:S(2)}) async-start(), calls=%async_computation.16 | async-start | bytes 10485760 | tf_op jit(solution)/shard_map/reduce_scatter | solution.py:20
  604.0 234.1 %reduce-scatter.22.cloned.1.call-start = ((), (), s32[]{:S(2)}) async-start(), calls=%async_computation.23 | async-start | bytes 5308416 | tf_op jit(solution)/shard_map/reduce_scatter | solution.py:147
  615.6 321.8 %reduce-scatter.24.cloned.1.call-start = ((), (), s32[]{:S(2)}) async-start(), calls=%async_computation.24 | async-start | bytes 5308416 | tf_op jit(solution)/shard_map/reduce_scatter | solution.py:148
  626.3 410.6 %reduce-scatter.26.cloned.1.call-start = ((), (), s32[]{:S(2)}) async-start(), calls=%async_computation.25 | async-start | bytes 5308416 | tf_op jit(solution)/shard_map/reduce_scatter | solution.py:149
  636.2 468.4 %reduce-scatter.20.cloned.1.call-start = ((), (), s32[]{:S(2)}) async-start(), calls=%async_computation.22 | async-start | bytes 1179648 | tf_op jit(solution)/shard_map/reduce_scatter | solution.py:146
  642.0 541.1 %reduce-scatter.18.cloned.1.call-start = ((), (), s32[]{:S(2)}) async-start(), calls=%async_computation.21 | async-start | bytes 3538944 | tf_op jit(solution)/shard_map/reduce_scatter | solution.py:145
  656.7 82.2 %copy-start = (f32[2048,256]{1,0:T(8,128)S(1)}, f32[2048,256]{1,0:T(8,128)}, u32[]{:S(2)}) copy-start(f32[2048,256]{1,0:T(8,128)} %get-tuple-element.23) | copy-start | bytes 6291460
  (13 other events, 75.9 us)
Sparse Core Ops, SparseCore 0:
  9.6 37.7 all-gather.8
  49.5 44.1 all-gather.10
  112.7 70.8 reduce-scatter.9
  185.8 52.0 all-gather.14
  240.0 33.5 all-gather.12
  275.8 52.0 all-gather.16
  330.1 52.2 all-gather.18
  384.0 33.2 all-gather.20
  451.9 71.6 reduce-scatter.13
  536.0 36.1 all-gather.22
  593.4 70.7 reduce-scatter.15
  666.9 71.9 reduce-scatter.11
  743.1 94.9 reduce-scatter.21
  842.2 95.1 reduce-scatter.23
  941.5 95.4 reduce-scatter.25
  1040.8 63.7 reduce-scatter.19
  1109.1 73.9 reduce-scatter.17
where the time goes:
time: 1200 us; the launch traced here: 1190 us
  waiting for transfers between devices  926 us (77%)
  matrix products  130 us (11%)
  blocking collectives  71.4 us (6%)
  other arithmetic  36.5 us (3%)
  between operations  14.5 us (1%)
    reduce_scatter x4, waiting for transfers between devices, sum_features(): return lax.psum_scatter(values, 'mp', scatter_dimension=1, tiled=True)  192 us
    all_gather x4, waiting for transfers between devices, collect_rows(): return lax.all_gather(values, 'mp', axis=1, tiled=True)  114 us
    reduce_scatter x1, waiting for transfers between devices, body(): lax.psum_scatter(grad_down, ('dp', 'tok'), scatter_dimension=1, tiled=True)  99.6 us
    reduce_scatter x1, waiting for transfers between devices, body(): lax.psum_scatter(grad_up, ('dp', 'tok'), scatter_dimension=0, tiled=True)  99.3 us
    reduce_scatter x1, waiting for transfers between devices, body(): lax.psum_scatter(grad_gate, ('dp', 'tok'), scatter_dimension=0, tiled=True)  94 us
    reduce_scatter x1, waiting for transfers between devices, body(): lax.psum_scatter(grad_in, ('dp', 'tok'), scatter_dimension=0, tiled=True)  78.4 us
    reduce_scatter x1, waiting for transfers between devices, body(): lax.psum_scatter(grad_out, ('dp', 'tok'), scatter_dimension=1, tiled=True)  67.6 us
    all_gather x1, waiting for transfers between devices, body(): lax.all_gather(down_weight, ('dp', 'tok'), axis=1, tiled=True)  44.3 us
  transfers between devices with their start and end apart: 19, of which 19 were waited for; matrix products, arithmetic and copies ran while one was open for 8% of the time, Pallas kernels for 0%

commit v1 on v0

--- a/solution.py
+++ b/solution.py
@@ -6,6 +6,28 @@
 eps_norm = 1e-05
 
 
+def joined_along(tiles, dim):
+    shape = list(tiles.shape[1:])
+    shape[dim] *= tiles.shape[0]
+    return jnp.moveaxis(tiles, 0, dim).reshape(shape)
+
+
+def doubled(array, axis):
+    devices = lax.axis_size(axis)
+    tiles = array[None]
+    for level in range(devices.bit_length() - 1):
+        bit = 1 << level
+        other = lax.ppermute(tiles, axis, [(i, i ^ bit) for i in range(devices)])
+        both = jnp.stack([tiles, other])
+        upper = lax.axis_index(axis) >> level & 1
+        tiles = jnp.where(upper == 0, both, both[::-1]).reshape(-1, *array.shape)
+    return tiles
+
+
+def doubled_up(value, axis, dim):
+    return joined_along(doubled(value, axis), dim)
+
+
 def passed_along(block, axis, distance):
     devices = range(lax.axis_size(axis))
     route = [(i - distance, i) for i in devices if i - distance in devices]
@@ -13,7 +35,7 @@
 
 
 def collect_rows(values):
-    return lax.all_gather(values, "mp", axis=1, tiled=True)
+    return doubled_up(values, "mp", 1)
 
 
 def sum_features(values):

time: 1200 us -> 1150 us (0.958)
  waiting for transfers between devices: 926 us -> 802 us
  local copies, waits for them, and re-layouts: 4.43 us -> 40.8 us
  other arithmetic: 36.5 us -> 58.7 us
    ppermute x0 -> x8, waiting for transfers between devices: none -> 145 us  [doubled(): other = lax.ppermute(tiles, axis, [(i, i ^ bit) for i in range(devices)])]
    all_gather x4 -> x0, waiting for transfers between devices: 114 us -> none  [collect_rows(): return lax.all_gather(values, 'mp', axis=1, tiled=True)]
    all_gather x1, waiting for transfers between devices: 44 us -> 0.01 us  [body(): lax.all_gather(up_weight, ('dp', 'tok'), axis=0, tiled=True)]
    all_gather x1, waiting for transfers between devices: 43.3 us -> 0.01 us  [body(): lax.all_gather(in_weight, ('dp', 'tok'), axis=0, tiled=True)]
    all_gather x1, waiting for transfers between devices: 39.8 us -> 0.01 us  [body(): lax.all_gather(gate_weight, ('dp', 'tok'), axis=0, tiled=True)]
    reduce_scatter x1, waiting for transfers between devices: 99.3 us -> 64.2 us  [body(): lax.psum_scatter(grad_up, ('dp', 'tok'), scatter_dimension=0, tiled=True)]
    reduce_scatter x4, waiting for transfers between devices: 192 us -> 220 us  [sum_features(): return lax.psum_scatter(values, 'mp', scatter_dimension=1, tiled=True)]
    all_gather x1, waiting for transfers between devices: 44.3 us -> 20.2 us  [body(): lax.all_gather(down_weight, ('dp', 'tok'), axis=1, tiled=True)]
  transfers between devices with their start and end apart: 19 -> 23, of which waited for: 19 -> 18; matrix products, arithmetic and copies ran while one was open for 8% -> 13% of each run, Pallas kernels for 0% -> 0%
where the time goes in v1:
time: 1150 us; the launch traced here: 1140 us
  waiting for transfers between devices  802 us (70%)
  matrix products  140 us (12%)
  blocking collectives  71.8 us (6%)
  other arithmetic  58.7 us (5%)
  local copies, waits for them, and re-layouts  40.8 us (4%)
  between operations  14.8 us (1%)
  starting transfers between devices  11.9 us (1%)
    reduce_scatter x4, waiting for transfers between devices, sum_features(): return lax.psum_scatter(values, 'mp', scatter_dimension=1, tiled=True)  220 us
    ppermute x8, waiting for transfers between devices, doubled(): other = lax.ppermute(tiles, axis, [(i, i ^ bit) for i in range(devices)])  145 us
    reduce_scatter x1, waiting for transfers between devices, body(): lax.psum_scatter(grad_down, ('dp', 'tok'), scatter_dimension=1, tiled=True)  99.9 us
    reduce_scatter x1, waiting for transfers between devices, body(): lax.psum_scatter(grad_gate, ('dp', 'tok'), scatter_dimension=0, tiled=True)  99.2 us
    reduce_scatter x1, waiting for transfers between devices, body(): lax.psum_scatter(grad_in, ('dp', 'tok'), scatter_dimension=0, tiled=True)  78.7 us
    reduce_scatter x1, waiting for transfers between devices, body(): lax.psum_scatter(grad_out, ('dp', 'tok'), scatter_dimension=1, tiled=True)  67.7 us
    reduce_scatter x1, waiting for transfers between devices, body(): lax.psum_scatter(grad_up, ('dp', 'tok'), scatter_dimension=0, tiled=True)  64.2 us
    all_gather x1, blocking collectives, body(): lax.all_gather(out_weight, ('dp', 'tok'), axis=1, tiled=True)  30.3 us
  transfers between devices with their start and end apart: 23, of which 18 were waited for; matrix products, arithmetic and copies ran while one was open for 13% of the time, Pallas kernels for 0%

profile of v1, /device:TPU:0, one launch (start us, length us, event | category | flops | bytes accessed | tf_op | source)
XLA Modules:
  0.0 1139.6 jit_solution(1431422176254735634)
XLA Ops:
  16.4 30.3 %all_gather.16 = bf16[256,1024]{1,0:T(8,128)(2,1)S(1)} all-gather(bf16[256,128]{1,0:T(8,128)(2,1)S(1)} %copy-done.13), channel_id=1, replica_groups=mesh['dp'=2,'tok'=4,'mp'=4] {'dp','tok'}, dimensions={1}, use_global_device_ids=true | all-gather | bytes 589824 | tf_op jit(solution)/shard_map/all_gather | solution.py:70
  46.7 15.8 %collective-permute-done.1 = bf16[2,2048,256]{2,1,0:T(8,128)(2,1)} collective-permute-done((bf16[2,2048,256]{2,1,0:T(8,128)(2,1)}, bf16[2,2048,256]{2,1,0:T(8,128)(2,1)}, u32[]{:S(2)}, u32[]{:S(2)}) %collective-permute-start.1) | collective-permute-done | bytes 2097184 | tf_op jit(solution)/shard_map/ppermute | solution.py:20
  65.3 13.5 %copy.24 = f32[4,2048,256]{2,0,1:T(4,128)S(1)} copy(f32[4,2048,256]{2,1,0:T(8,128)S(1)} %bitcast.129) | data formatting | bytes 16777216 | tf_op jit(solution)/shard_map/convert_element_type | solution.py:76
  108.3 71.6 %reduce-scatter.10.cloned.1.call-done = f32[2048,256]{1,0:T(8,128)} async-done(((f32[2048,1024]{1,0:T(8,128)}), f32[2048,256]{1,0:T(8,128)}) %reduce-scatter.10.cloned.1.call-update) | async-done | bytes 2097168 | tf_op jit(solution)/shard_map/reduce_scatter | solution.py:42
  200.2 44.0 %collective-permute-done.6 = bf16[2,2048,256]{2,1,0:T(8,128)(2,1)} collective-permute-done((bf16[2,2048,256]{2,1,0:T(8,128)(2,1)}, bf16[2,2048,256]{2,1,0:T(8,128)(2,1)}, u32[]{:S(2)}, u32[]{:S(2)}) %collective-permute-start.6) | collective-permute-done | bytes 2097184 | tf_op jit(solution)/shard_map/ppermute | solution.py:20
  256.1 32.6 %collective-permute-done.4 = bf16[2,2048,256]{2,1,0:T(8,128)(2,1)} collective-permute-done((bf16[2,2048,256]{2,1,0:T(8,128)(2,1)}, bf16[2,2048,256]{2,1,0:T(8,128)(2,1)}, u32[]{:S(2)}, u32[]{:S(2)}) %collective-permute-start.4) | collective-permute-done | bytes 2097184 | tf_op jit(solution)/shard_map/ppermute | solution.py:20
  300.7 10.4 fusion.27
  311.0 10.3 fusion.28
  321.3 20.2 %all-gather.11.cloned.1.call-done = bf16[1152,1024]{1,0:T(8,128)(2,1)} async-done(((bf16[1152,128]{1,0:T(8,128)(2,1)}), bf16[1152,1024]{1,0:T(8,128)(2,1)}) %all-gather.11.cloned.1.call-update) | async-done | bytes 2359312 | tf_op jit(solution)/shard_map/all_gather | solution.py:73
  341.5 18.4 %multiply_convert_fusion = (bf16[2048,1152]{1,0:T(8,128)(2,1)}, bf16[2048,1152]{1,0:T(8,128)(2,1)}, bf16[2048,1152]{1,0:T(8,128)(2,1)}) fusion(f32[2048,1152]{1,0:T(8,128)} %fusion.27, f32[2048,1152]{1,0:T(8,128)} %fusion.28, bf16[2048,1024]{0,1:T(8,128)(2,1)} %bitcast.135, bf16[1152,1024]{1,0:T(8,128)(2,1)} %all-gather.11.cloned.1.call-done), kind=kOutput, calls=%fused_computation | convolution fusion | flops 4867227648 | bytes 39583744 | tf_op jit(solution)/shard_map/td,fd->tf/dot_general | solution.py:113
  359.9 16.2 %fusion.30 = f32[2048,1024]{1,0:T(8,128)S(1)} fusion(bf16[2048,1152]{1,0:T(8,128)(2,1)} %get-tuple-element.29, bf16[1024,1152]{1,0:T(8,128)(2,1)S(1)} %copy-done.17), kind=kOutput, calls=%fused_computation.87 | convolution fusion | flops 4831838208 | bytes 15466496 | tf_op jit(solution)/shard_map/tf,df->td/dot_general | solution.py:119
  384.5 10.6 fusion.29
  395.2 59.3 %reduce-scatter.14.cloned.1.call-done = f32[2048,256]{1,0:T(8,128)} async-done(((f32[2048,1024]{1,0:T(8,128)}), f32[2048,256]{1,0:T(8,128)}) %reduce-scatter.14.cloned.1.call-update) | async-done | bytes 2097168 | tf_op jit(solution)/shard_map/reduce_scatter | solution.py:42
  463.4 65.5 %reduce-scatter.12.cloned.1.call-done = f32[2048,256]{1,0:T(8,128)} async-done(((f32[2048,1024]{1,0:T(8,128)}), f32[2048,256]{1,0:T(8,128)}) %reduce-scatter.12.cloned.1.call-update) | async-done | bytes 2097168 | tf_op jit(solution)/shard_map/reduce_scatter | solution.py:42
  538.2 47.3 %collective-permute-done.8 = bf16[2,2048,256]{2,1,0:T(8,128)(2,1)S(1)} collective-permute-done((bf16[2,2048,256]{2,1,0:T(8,128)(2,1)S(1)}, bf16[2,2048,256]{2,1,0:T(8,128)(2,1)S(1)}, u32[]{:S(2)}, u32[]{:S(2)}) %collective-permute-start.8) | collective-permute-done | bytes 2097184 | tf_op jit(solution)/shard_map/ppermute | solution.py:20
  626.6 11.6 %fusion.33 = f32[1024,1152]{1,0:T(8,128)} fusion(bf16[2048,1024]{0,1:T(8,128)(2,1)} %bitcast.140, bf16[2048,1152]{1,0:T(8,128)(2,1)} %get-tuple-element.29), kind=kOutput, calls=%fused_computation.90 | convolution fusion | flops 4831838208 | bytes 13631488 | tf_op jit(solution)/shard_map/td,tf->df/dot_general | solution.py:117
  638.3 10.3 fusion.35
  663.6 23.7 %reduce-scatter.16.cloned.1.call-done = f32[2048,256]{1,0:T(8,128)} async-done(((f32[2048,1024]{1,0:T(8,128)}), f32[2048,256]{1,0:T(8,128)}) %reduce-scatter.16.cloned.1.call-update) | async-done | bytes 2097168 | tf_op jit(solution)/shard_map/reduce_scatter | solution.py:42
  690.0 23.2 %all-reduce = (f32[3,256]{1,0:T(4,128)}, f32[256]{0:T(256)}, f32[256]{0:T(256)}) all-reduce(f32[3,256]{1,0:T(4,128)S(1)} %pad_maximum_fusion.11, f32[256]{0:T(256)S(1)} %get-tuple-element.10, f32[256]{0:T(256)S(1)} %get-tuple-element.15), channel_id=1, replica_groups=mesh['dp'=2,'tok'=4,'mp'=4] {'dp','tok'}, use_global_device_ids=true, to_apply=%region_15.16 | all-reduce | flops 1280 | bytes 10240 | tf_op jit(solution)/shard_map/psum | solution.py:163
  723.0 64.2 %reduce-scatter.24.cloned.1.call-done = f32[128,1152]{1,0:T(8,128)} async-done(((f32[1024,1152]{1,0:T(8,128)}), f32[128,1152]{1,0:T(8,128)}) %reduce-scatter.24.cloned.1.call-update) | async-done | bytes 589840 | tf_op jit(solution)/shard_map/reduce_scatter | solution.py:170
  787.2 99.2 %reduce-scatter.22.cloned.1.call-done = f32[128,1152]{1,0:T(8,128)} async-done(((f32[1024,1152]{1,0:T(8,128)}), f32[128,1152]{1,0:T(8,128)}) %reduce-scatter.22.cloned.1.call-update) | async-done | bytes 589840 | tf_op jit(solution)/shard_map/reduce_scatter | solution.py:169
  886.4 99.9 %reduce-scatter.26.cloned.1.call-done = f32[1152,128]{1,0:T(8,128)} async-done(((f32[1152,1024]{1,0:T(8,128)}), f32[1152,128]{1,0:T(8,128)}) %reduce-scatter.26.cloned.1.call-update) | async-done | bytes 589840 | tf_op jit(solution)/shard_map/reduce_scatter | solution.py:171
  986.3 67.7 %reduce-scatter.20.cloned.1.call-done = f32[256,128]{1,0:T(8,128)} async-done(((f32[256,1024]{1,0:T(8,128)}), f32[256,128]{1,0:T(8,128)}) %reduce-scatter.20.cloned.1.call-update) | async-done | bytes 131088 | tf_op jit(solution)/shard_map/reduce_scatter | solution.py:168
  1053.9 78.7 %reduce-scatter.18.cloned.1.call-done = f32[128,3,256]{2,0,1:T(8,128)} async-done(((f32[1024,3,256]{2,0,1:T(8,128)}), f32[128,3,256]{2,0,1:T(8,128)}) %reduce-scatter.18.cloned.1.call-update) | async-done | bytes 393232 | tf_op jit(solution)/shard_map/reduce_scatter | solution.py:167
  (149 shorter events, 180.3 us)
Async XLA Ops:
  7.2 79.5 %all-gather.5.cloned.1.call-start = ((), (), s32[]{:S(2)}) async-start(), calls=%async_computation.9 | async-start | bytes 1769472 | tf_op jit(solution)/shard_map/all_gather | solution.py:69
  7.2 3.0 collective-permute-start
  13.5 49.1 %collective-permute-start.1 = (bf16[2,2048,256]{2,1,0:T(8,128)(2,1)}, bf16[2,2048,256]{2,1,0:T(8,128)(2,1)}, u32[]{:S(2)}, u32[]{:S(2)}) collective-permute-start(bf16[2,2048,256]{2,1,0:T(8,128)(2,1)} %get-tuple-element.45), channel_id=1, source_target_pairs={{0,2},{1,3},{2,0},{3,1},{4,6},{5,7},{6,4},{7,5},{8,10},{9,11},{10,... | collective-permute-start | bytes 6291464 | tf_op jit(solution)/shard_map/ppermute | solution.py:20
  16.4 163.5 %reduce-scatter.10.cloned.1.call-start = ((), (), s32[]{:S(2)}) async-start(), calls=%async_computation.10 | async-start | bytes 10485760 | tf_op jit(solution)/shard_map/reduce_scatter | solution.py:42
  93.3 5.0 collective-permute-start.2
  106.0 73.9 %copy-start.6 = (bf16[2048,256]{1,0:T(8,128)(2,1)S(1)}, bf16[2048,256]{1,0:T(8,128)(2,1)}, u32[]{:S(2)}) copy-start(bf16[2048,256]{1,0:T(8,128)(2,1)} %param.10) | copy-start | bytes 3145732
  106.1 194.6 %all-gather.7.cloned.1.call-start = ((), (), s32[]{:S(2)}) async-start(), calls=%async_computation.11 | async-start | bytes 2654208 | tf_op jit(solution)/shard_map/all_gather | solution.py:71
  106.8 204.2 %all-gather.9.cloned.1.call-start = ((), (), s32[]{:S(2)}) async-start(), calls=%async_computation.12 | async-start | bytes 2654208 | tf_op jit(solution)/shard_map/all_gather | solution.py:72
  107.4 234.1 %all-gather.11.cloned.1.call-start = ((), (), s32[]{:S(2)}) async-start(), calls=%async_computation.13 | async-start | bytes 2654208 | tf_op jit(solution)/shard_map/all_gather | solution.py:73
  107.4 84.1 %collective-permute-start.5 = (bf16[1,2048,256]{2,1,0:T(8,128)(2,1)}, bf16[1,2048,256]{2,1,0:T(8,128)(2,1)}, u32[]{:S(2)}, u32[]{:S(2)}) collective-permute-start(bf16[1,2048,256]{2,1,0:T(8,128)(2,1)} %bitcast.145), channel_id=1, source_target_pairs={{0,1},{1,0},{2,3},{3,2},{4,5},{5,4},{6,7},{7,6},{8,9},{9,8},{10,11... | collective-permute-start | bytes 3145736 | tf_op jit(solution)/shard_map/ppermute | solution.py:20
  191.4 5.8 collective-permute-start.3
  195.5 48.7 %collective-permute-start.6 = (bf16[2,2048,256]{2,1,0:T(8,128)(2,1)}, bf16[2,2048,256]{2,1,0:T(8,128)(2,1)}, u32[]{:S(2)}, u32[]{:S(2)}) collective-permute-start(bf16[2,2048,256]{2,1,0:T(8,128)(2,1)} %get-tuple-element.41), channel_id=1, source_target_pairs={{0,2},{1,3},{2,0},{3,1},{4,6},{5,7},{6,4},{7,5},{8,10},{9,11},{10,... | collective-permute-start | bytes 6291464 | tf_op jit(solution)/shard_map/ppermute | solution.py:20
  199.8 88.9 %collective-permute-start.4 = (bf16[2,2048,256]{2,1,0:T(8,128)(2,1)}, bf16[2,2048,256]{2,1,0:T(8,128)(2,1)}, u32[]{:S(2)}, u32[]{:S(2)}) collective-permute-start(bf16[2,2048,256]{2,1,0:T(8,128)(2,1)} %get-tuple-element.43), channel_id=1, source_target_pairs={{0,2},{1,3},{2,0},{3,1},{4,6},{5,7},{6,4},{7,5},{8,10},{9,11},{10,... | collective-permute-start | bytes 6291464 | tf_op jit(solution)/shard_map/ppermute | solution.py:20
  200.2 254.4 %reduce-scatter.14.cloned.1.call-start = ((), (), s32[]{:S(2)}) async-start(), calls=%async_computation.15 | async-start | bytes 10485760 | tf_op jit(solution)/shard_map/reduce_scatter | solution.py:42
  384.5 144.4 %reduce-scatter.12.cloned.1.call-start = ((), (), s32[]{:S(2)}) async-start(), calls=%async_computation.14 | async-start | bytes 10485760 | tf_op jit(solution)/shard_map/reduce_scatter | solution.py:42
  395.2 292.1 %reduce-scatter.16.cloned.1.call-start = ((), (), s32[]{:S(2)}) async-start(), calls=%async_computation.16 | async-start | bytes 10485760 | tf_op jit(solution)/shard_map/reduce_scatter | solution.py:42
  534.4 2.7 collective-permute-start.7
  537.8 47.7 %collective-permute-start.8 = (bf16[2,2048,256]{2,1,0:T(8,128)(2,1)S(1)}, bf16[2,2048,256]{2,1,0:T(8,128)(2,1)S(1)}, u32[]{:S(2)}, u32[]{:S(2)}) collective-permute-start(bf16[2,2048,256]{2,1,0:T(8,128)(2,1)S(1)} %get-tuple-element.38), channel_id=1, source_target_pairs={{0,2},{1,3},{2,0},{3,1},{4,6},{5,7},{6,4},{7,5},{8,10},{9,11},{10,... | collective-permute-start | bytes 6291464 | tf_op jit(solution)/shard_map/ppermute | solution.py:20
  601.2 5.6 collective-permute-start.9
  616.3 170.8 %reduce-scatter.24.cloned.1.call-start = ((), (), s32[]{:S(2)}) async-start(), calls=%async_computation.20 | async-start | bytes 5308416 | tf_op jit(solution)/shard_map/reduce_scatter | solution.py:170
  626.6 259.8 %reduce-scatter.22.cloned.1.call-start = ((), (), s32[]{:S(2)}) async-start(), calls=%async_computation.19 | async-start | bytes 5308416 | tf_op jit(solution)/shard_map/reduce_scatter | solution.py:169
  638.2 348.1 %reduce-scatter.26.cloned.1.call-start = ((), (), s32[]{:S(2)}) async-start(), calls=%async_computation.21 | async-start | bytes 5308416 | tf_op jit(solution)/shard_map/reduce_scatter | solution.py:171
  648.6 405.4 %reduce-scatter.20.cloned.1.call-start = ((), (), s32[]{:S(2)}) async-start(), calls=%async_computation.18 | async-start | bytes 1179648 | tf_op jit(solution)/shard_map/reduce_scatter | solution.py:168
  654.3 478.4 %reduce-scatter.18.cloned.1.call-start = ((), (), s32[]{:S(2)}) async-start(), calls=%async_computation.17 | async-start | bytes 3538944 | tf_op jit(solution)/shard_map/reduce_scatter | solution.py:167
  (22 other events, 282.2 us)
Sparse Core Ops, SparseCore 0:
  16.5 46.2 all-gather.4
  106.2 73.6 reduce-scatter.9
  182.2 52.0 all-gather.6
  236.5 50.6 all-gather.8
  289.1 52.2 all-gather.10
  384.6 69.9 reduce-scatter.13
  457.1 71.7 reduce-scatter.11
  616.5 70.7 reduce-scatter.15
  691.5 95.6 reduce-scatter.23
  791.2 95.1 reduce-scatter.21
  890.6 95.5 reduce-scatter.25
  990.1 63.7 reduce-scatter.19
  1058.6 74.0 reduce-scatter.17
